TPU v7x, 32 devices: a whole 2x2x4 slice. The times are simulated.
32 devices in a mesh: tensor: 4 (over z), example: 8 (over y, x, core).
Axes of the slice: x: 2, y: 2, z: 4, core: 2. Of those that a mesh axis runs over, the one named last changes fastest.
Arguments:
- queries: bfloat16 [1, 4096, 4096], P(None, 'example', 'tensor'), may hold values from -0.0014648438 to 0.0014648438
- basis_out: bfloat16 [4096, 4096], P('example', 'tensor'), may hold values from -0.09375 to 0.09375
- basis_in: bfloat16 [4096, 4096], P('tensor', 'example'), may hold values from -0.09375 to 0.09375
- eigvals: float32 [4096, 4096], P('tensor', 'example'), may hold values from 0.25 to 4
- input_fac: bfloat16 [128, 8, 4096], P('example', None, 'tensor'), may hold values from -6 to 6
- grad_fac: bfloat16 [128, 8, 4096], P('example', None, 'tensor'), may hold values from -6 to 6
- cand_slot: int32 [128], replicated, may hold values from 0 to 127, as said below
- score_list: int32 [8, 16], replicated, may hold values from 0 to 127, as said below
- token_count: int32 [128], replicated, may hold values from 1 to 8
Outputs:
- scores: float32 [1, 128, 8], P(None, 'example')
Inputs may be any that keep to these rules, and one draw needn't show every extreme that they name: `cand_slot`: a permutation; slot s belongs to owner s // 16. `score_list`: every candidate appears exactly once; a scorer's list holds at most 4 candidates of any one owner, and some scorer takes exactly 4 from some owner.
All inputs are finite; a program needn't handle non-finite values.
Results may differ from a plain program's by a relative error of at most 0.019.
Values may be sent and summed in bfloat16 or wider, within the bound.
A program may use at most 128 MiB of HBM per device.

v0:
```python
import jax
import jax.numpy as jnp
from jax import lax
from jax.sharding import PartitionSpec as P

BF = jnp.bfloat16
F32 = jnp.float32


def regroup_grads(grads, n_tensor, n_example):
    ratio = n_example // n_tensor
    half = grads.shape[1] // ratio
    parity = lax.axis_index("example") % ratio
    received = []
    for shift in range(ratio):
        piece = lax.dynamic_slice_in_dim(grads, (parity + shift) % ratio * half, half, 1)
        perm = []
        for t in range(n_tensor):
            for e in range(n_example):
                target = e // ratio * n_example + ratio * t + (e + shift) % ratio
                perm.append((t * n_example + e, target))
        received.append(lax.ppermute(piece, ("tensor", "example"), perm))
    stacked = jnp.stack(received)
    order = (parity - jnp.arange(ratio)) % ratio
    pieces = [lax.dynamic_index_in_dim(stacked, order[p], 0, keepdims=False) for p in range(ratio)]
    return jnp.concatenate(pieces, axis=0)


def body(
    queries, basis_out, basis_in, eigvals, input_fac, grad_fac, cand_slot, score_list, token_count
):
    n_example = lax.axis_size("example")
    n_tensor = lax.axis_size("tensor")
    my_index = lax.axis_index("example")
    cand_total = cand_slot.shape[0]
    token_len = input_fac.shape[1]
    list_len = score_list.shape[1]
    query_total, rows, width = queries.shape
    acts = input_fac.reshape(-1, width)
    grads = grad_fac.reshape(-1, width)
    tokens = acts.shape[0]
    in_rows = lax.all_gather(basis_in, "example", axis=1, tiled=True)
    moved_grads = regroup_grads(grads, n_tensor, n_example)
    out_rows = lax.all_gather(basis_out, "tensor", axis=1, tiled=True)
    left = jnp.concatenate([queries.reshape(-1, width), acts], axis=0)
    half_rotated = lax.psum_scatter(
        jnp.einsum("jl,rj->lr", in_rows, left, preferred_element_type=F32).astype(BF),
        "tensor",
        scatter_dimension=0,
        tiled=True,
    )
    split = query_total * rows
    acts_rot = lax.all_gather(half_rotated[:, split:], "example", axis=0)
    parts = [half_rotated[:, q * rows : (q + 1) * rows] for q in range(query_total)]
    right = jnp.concatenate(parts + [moved_grads], axis=0)
    core = lax.psum_scatter(
        jnp.einsum("ik,xi->kx", out_rows, right, preferred_element_type=F32).astype(BF),
        "example",
        scatter_dimension=0,
        tiled=True,
    )
    wide = half_rotated.shape[0]
    grads_rot = lax.all_gather(core[:, query_total * wide :], "tensor", axis=0)
    acts_flat = jnp.transpose(acts_rot, (1, 0, 2)).reshape(wide, -1).astype(F32)
    grads_flat = jnp.transpose(grads_rot, (1, 0, 2)).reshape(core.shape[0], -1)
    partial = []
    for q in range(query_total):
        scaled = (core[:, q * wide : (q + 1) * wide].astype(F32) / eigvals.T).astype(BF)
        weighted = jnp.einsum("kl,kt->lt", scaled, grads_flat, preferred_element_type=F32)
        partial.append(jnp.sum(weighted * acts_flat, axis=0))
    summed = lax.psum(jnp.stack(partial), ("tensor", "example"))
    by_slot = summed.reshape(query_total, cand_total, token_len)
    my_list = lax.dynamic_index_in_dim(score_list, my_index, 0, keepdims=False)
    ids = jnp.arange(cand_total, dtype=jnp.int32)
    matches = my_list[:, None] == ids[None, :]
    my_slot = jnp.sum(jnp.where(matches, cand_slot[None, :], 0), axis=1)
    my_count = jnp.sum(jnp.where(matches, token_count[None, :], 0), axis=1)
    pick = my_slot[:, None] == ids[None, :]
    scores = jnp.sum(jnp.where(pick[None, :, :, None], by_slot[:, None], F32(0.0)), axis=2)
    live = jnp.arange(token_len, dtype=jnp.int32)[None, :] < my_count[:, None]
    return jnp.where(live[None], scores, F32(0.0))


def solution(mesh):
    in_specs = (
        P(None, "example", "tensor"),
        P("example", "tensor"),
        P("tensor", "example"),
        P("tensor", "example"),
        P("example", None, "tensor"),
        P("example", None, "tensor"),
        P(),
        P(),
        P(),
    )
    out_specs = P(None, "example", None)
    return jax.shard_map(body, mesh=mesh, in_specs=in_specs, out_specs=out_specs, check_vma=False)
```

profile of v0, /device:TPU:0, one launch (start us, length us, event | category | flops | bytes accessed | tf_op | source)
XLA Modules:
  0.0 471.9 jit_solution(15291793643969894554)
XLA Ops:
  6.5 0.0 copy-start
  6.5 0.0 all-gather.7.cloned.1.call-start
  6.5 0.7 all-gather.7.cloned.1.call-update
  7.3 0.0 reduce-scatter.3.cloned.1.call-start
  7.3 60.6 %all-gather.7.cloned.1.call-done = bf16[1024,4096]{1,0:T(8,128)(2,1)} async-done(((bf16[1024,512]{1,0:T(8,128)(2,1)}), bf16[1024,4096]{1,0:T(8,128)(2,1)}) %all-gather.7.cloned.1.call-update) | async-done | bytes 8388624 | tf_op jit(solution)/shard_map/all_gather | solution.py:42
  67.9 9.9 %fusion.1 = bf16[4096,640]{0,1:T(8,128)(2,1)} fusion(bf16[1024,4096]{1,0:T(8,128)(2,1)} %all-gather.7.cloned.1.call-done, bf16[128,1024]{1,0:T(8,128)(2,1)} %bitcast.54, bf16[512,1024]{1,0:T(8,128)(2,1)} %bitcast.53), kind=kOutput, calls=%fused_computation.3 | convolution fusion | flops 5373952000 | bytes 14942208 | tf_op jit(solution)/shard_map/jl,rj->lr/dot_general | solution.py:47
  77.8 0.0 reduce-scatter.3.cloned.1.call-update
  77.8 0.0 all-gather.9.cloned.1.call-start
  77.9 0.7 all-gather.9.cloned.1.call-update
  78.6 0.0 reduce-scatter.5.cloned.1.call-start
  78.7 0.1 copy-done.1
  78.8 0.1 copy.23
  78.9 0.7 collective-permute-start
  79.6 0.1 copy.24
  79.7 0.3 collective-permute-start.1
  80.0 0.6 fusion.22
  84.5 0.0 collective-permute-done
  84.5 0.0 collective-permute-done.1
  84.5 0.1 fusion.17
  84.6 102.3 %reduce-scatter.3.cloned.1.call-done = bf16[1024,640]{0,1:T(8,128)(2,1)} async-done(((bf16[4096,640]{0,1:T(8,128)(2,1)}), bf16[1024,640]{0,1:T(8,128)(2,1)}) %reduce-scatter.3.cloned.1.call-update) | async-done | bytes 1310736 | tf_op jit(solution)/shard_map/reduce_scatter | solution.py:46
  186.9 1.3 slice.24
  188.2 80.4 %all-gather.9.cloned.1.call-done = bf16[512,4096]{1,0:T(8,128)(2,1)} async-done(((bf16[512,1024]{1,0:T(8,128)(2,1)}), bf16[512,4096]{1,0:T(8,128)(2,1)}) %all-gather.9.cloned.1.call-update) | async-done | bytes 4194320 | tf_op jit(solution)/shard_map/all_gather | solution.py:44
  268.6 10.5 %fusion = bf16[4096,1280]{0,1:T(8,128)(2,1)} fusion(bf16[512,4096]{1,0:T(8,128)(2,1)} %all-gather.9.cloned.1.call-done, bf16[128,512]{0,1:T(8,128)(2,1)S(1)} %get-tuple-element.8, bf16[128,512]{0,1:T(8,128)(2,1)S(1)} %get-tuple-element.7, bf16[1024,512]{0,1:T(8,128)(2,1)S(1)} %slice.24), kind=kOutput, calls=%fused_computation.1 | convolution fusion | flops 5377884160 | bytes 15990784 | tf_op jit(solution)/shard_map/ik,xi->kx/dot_general | solution.py:57
  279.1 0.0 reduce-scatter.5.cloned.1.call-update
  279.2 0.0 all-gather.13.cloned.1.call-start
  279.2 1.7 slice.27
  280.9 0.0 all-gather.13.cloned.1.call-update
  280.9 0.2 all-gather.11.cloned.1.call-start
  281.2 78.3 %reduce-scatter.5.cloned.1.call-done = bf16[512,1280]{0,1:T(8,128)(2,1)} async-done(((bf16[4096,1280]{0,1:T(8,128)(2,1)}), bf16[512,1280]{0,1:T(8,128)(2,1)}) %reduce-scatter.5.cloned.1.call-update) | async-done | bytes 1310736 | tf_op jit(solution)/shard_map/reduce_scatter | solution.py:56
  359.4 1.7 slice.26
  361.1 0.0 all-gather.11.cloned.1.call-update
  361.1 0.0 copy-done
  361.1 0.0 copy-done.3
  361.1 0.0 copy-done.4
  361.1 0.2 select_reduce_fusion.2
  361.3 0.1 iota_compare_fusion
  361.4 27.7 %all-gather.13.cloned.1.call-done = bf16[8192,128]{0,1:T(8,128)(2,1)} async-done(((bf16[1024,128]{0,1:T(8,128)(2,1)}), bf16[8192,128]{0,1:T(8,128)(2,1)}) %all-gather.13.cloned.1.call-update) | async-done | bytes 2097168 | tf_op jit(solution)/shard_map/all_gather | solution.py:53
  389.1 2.0 convert_element_type.38
  391.1 5.3 %copy.26 = f32[16,8,8,1024]{3,2,1,0:T(8,128)} copy(f32[16,8,8,1024]{3,1,2,0:T(8,128)S(1)} %bitcast.45) | data formatting | bytes 8388608
  396.4 5.9 %copy.20 = f32[1024,8,128]{2,1,0:T(8,128)} copy(f32[1024,8,128]{0,1,2:T(8,128)} %bitcast.46) | data formatting | bytes 8388608 | tf_op jit(solution)/shard_map/convert_element_type | solution.py:64
  402.4 16.1 %all-gather.11.cloned.1.call-done = bf16[2048,256]{0,1:T(8,128)(2,1)} async-done(((bf16[512,256]{0,1:T(8,128)(2,1)}), bf16[2048,256]{0,1:T(8,128)(2,1)}) %all-gather.11.cloned.1.call-update) | async-done | bytes 1048592 | tf_op jit(solution)/shard_map/all_gather | solution.py:63
  418.5 1.3 copy.30
  419.8 3.9 fusion.2
  423.7 0.1 broadcast_in_dim.58
  423.8 40.5 %psum.7 = f32[128,8]{1,0:T(8,128)S(1)} all-reduce(f32[128,8]{1,0:T(8,128)S(1)} %broadcast_in_dim.58), channel_id=1, replica_groups=mesh['tensor'=4,'example'=8] {'tensor','example'}, use_global_device_ids=true, to_apply=%region_5.6 | all-reduce | flops 1024 | bytes 8192 | tf_op jit(solution)/shard_map/psum | solution.py:71
  464.3 0.1 select_reduce_fusion
  464.4 0.1 copy.22
  464.5 0.6 bitcast_select_fusion
  (11 shorter events, 0.1 us)
Async XLA Ops:
  6.5 354.6 %copy-start = (s32[8,16]{1,0:T(8,128)S(1)}, s32[8,16]{1,0:T(8,128)}, u32[]{:S(2)}) copy-start(s32[8,16]{1,0:T(8,128)} %param.16) | copy-start | bytes 1540
  6.5 61.4 %all-gather.7.cloned.1.call-start = ((), (), s32[]{:S(2)}) async-start(), calls=%async_computation.2 | async-start | bytes 9437184 | tf_op jit(solution)/shard_map/all_gather | solution.py:42
  7.3 179.7 %reduce-scatter.3.cloned.1.call-start = ((), (), s32[]{:S(2)}) async-start(), calls=%async_computation.3 | async-start | bytes 6553600 | tf_op jit(solution)/shard_map/reduce_scatter | solution.py:46
  77.8 0.9 copy-start.1
  77.8 190.8 %all-gather.9.cloned.1.call-start = ((), (), s32[]{:S(2)}) async-start(), calls=%async_computation.4 | async-start | bytes 5242880 | tf_op jit(solution)/shard_map/all_gather | solution.py:44
  78.6 280.9 %reduce-scatter.5.cloned.1.call-start = ((), (), s32[]{:S(2)}) async-start(), calls=%async_computation.5 | async-start | bytes 11796480 | tf_op jit(solution)/shard_map/reduce_scatter | solution.py:56
  78.9 5.6 %collective-permute-start = (bf16[128,512]{0,1:T(8,128)(2,1)S(1)}, bf16[128,512]{0,1:T(8,128)(2,1)S(1)}, u32[]{:S(2)}, u32[]{:S(2)}) collective-permute-start(bf16[128,512]{0,1:T(8,128)(2,1)S(1)} %copy.23), channel_id=1, source_target_pairs={{0,0},{1,1},{2,8},{3,9},{4,16},{5,17},{6,24},{7,25},{8,2},{9,3},{1... | collective-permute-start | bytes 393224 | tf_op jit(solution)/shard_map/ppermute | solution.py:22
  79.7 4.8 %collective-permute-start.1 = (bf16[128,512]{0,1:T(8,128)(2,1)S(1)}, bf16[128,512]{0,1:T(8,128)(2,1)S(1)}, u32[]{:S(2)}, u32[]{:S(2)}) collective-permute-start(bf16[128,512]{0,1:T(8,128)(2,1)S(1)} %copy.24), channel_id=1, source_target_pairs={{0,1},{1,0},{2,9},{3,8},{4,17},{5,16},{6,25},{7,24},{8,3},{9,2},{1... | collective-permute-start | bytes 393224 | tf_op jit(solution)/shard_map/ppermute | solution.py:22
  279.1 82.0 %copy-start.3 = (s32[128]{0:T(128)S(1)}, s32[128]{0:T(128)}, u32[]{:S(2)}) copy-start(s32[128]{0:T(128)} %param.17) | copy-start | bytes 1540
  279.1 82.0 %copy-start.4 = (s32[128]{0:T(128)S(1)}, s32[128]{0:T(128)}, u32[]{:S(2)}) copy-start(s32[128]{0:T(128)} %param.15) | copy-start | bytes 1540
  279.2 109.9 %all-gather.13.cloned.1.call-start = ((), (), s32[]{:S(2)}) async-start(), calls=%async_computation.7 | async-start | bytes 2359296 | tf_op jit(solution)/shard_map/all_gather | solution.py:53
  280.9 137.5 %all-gather.11.cloned.1.call-start = ((), (), s32[]{:S(2)}) async-start(), calls=%async_computation.6 | async-start | bytes 1310720 | tf_op jit(solution)/shard_map/all_gather | solution.py:63
  396.4 23.4 %copy-start.2 = (bf16[512,1280]{0,1:T(8,128)(2,1)S(1)}, bf16[512,1280]{0,1:T(8,128)(2,1)}, u32[]{:S(2)}) copy-start(bf16[512,1280]{0,1:T(8,128)(2,1)} %reduce-scatter.5.cloned.1.call-done) | copy-start | bytes 3932164
  396.4 23.4 %copy-start.5 = (f32[1024,512]{1,0:T(8,128)S(1)}, f32[1024,512]{1,0:T(8,128)}, u32[]{:S(2)}) copy-start(f32[1024,512]{1,0:T(8,128)} %param.12) | copy-start | bytes 6291460
Sparse Core Ops, SparseCore 0:
  9.2 58.6 all-gather.6
  77.9 108.9 reduce-scatter.2
  188.5 80.0 all-gather.8
  279.3 80.0 reduce-scatter.4
  361.2 27.8 all-gather.12
  390.5 27.9 all-gather.10
where the time goes:
time: 472 us
  waiting for transfers between devices  367 us (78%)
  blocking collectives  40.5 us (9%)
  matrix products  24.3 us (5%)
  local copies, waits for them, and re-layouts  18.4 us (4%)
  between operations  17.5 us (4%)
    reduce_scatter x1, waiting for transfers between devices, body(): lax.psum_scatter(jnp.einsum('jl,rj->lr', in_rows, left, preferred_element...  102 us
    all_gather x1, waiting for transfers between devices, body(): out_rows = lax.all_gather(basis_out, 'tensor', axis=1, tiled=True)  80.4 us
    reduce_scatter x1, waiting for transfers between devices, body(): lax.psum_scatter(jnp.einsum('ik,xi->kx', out_rows, right, preferred_eleme...  78.3 us
    all_gather x1, waiting for transfers between devices, body(): in_rows = lax.all_gather(basis_in, 'example', axis=1, tiled=True)  60.6 us
    psum x1, blocking collectives, body(): summed = lax.psum(jnp.stack(partial), ('tensor', 'example'))  40.5 us
    all_gather x1, waiting for transfers between devices, body(): acts_rot = lax.all_gather(half_rotated[:, split:], 'example', axis=0)  27.7 us
    all_gather x1, waiting for transfers between devices, body(): grads_rot = lax.all_gather(core[:, query_total * wide:], 'tensor', axis=0)  16.1 us
    dot_general x1, matrix products, body(): jnp.einsum('ik,xi->kx', out_rows, right, preferred_element_type=F32)  10.5 us
  transfers between devices with their start and end apart: 8, of which 6 were waited for; matrix products, arithmetic and copies ran while one was open for 4% of the time, Pallas kernels for 0%

commit v1 on v0

--- a/solution.py
+++ b/solution.py
@@ -41,7 +41,14 @@
     tokens = acts.shape[0]
     in_rows = lax.all_gather(basis_in, "example", axis=1, tiled=True)
     moved_grads = regroup_grads(grads, n_tensor, n_example)
-    out_rows = lax.all_gather(basis_out, "tensor", axis=1, tiled=True)
+    ring = [basis_out]
+    for hop in range(3):
+        ring.append(lax.ppermute(ring[-1], "tensor", [(dev, (dev + 1) % 4) for dev in range(4)]))
+    out_rows = jnp.roll(
+        jnp.concatenate(ring[::-1], axis=1),
+        (lax.axis_index("tensor") + 1) * ring[0].shape[1],
+        axis=1,
+    )
     left = jnp.concatenate([queries.reshape(-1, width), acts], axis=0)
     half_rotated = lax.psum_scatter(
         jnp.einsum("jl,rj->lr", in_rows, left, preferred_element_type=F32).astype(BF),

time: 472 us -> 470 us (level)
  waiting for transfers between devices: 367 us -> 311 us
  starting transfers between devices: 1.38 us -> 37.9 us
  local copies, waits for them, and re-layouts: 18.4 us -> 33.3 us
    ppermute x0 -> x3, waiting for transfers between devices: none -> 113 us  [body(): lax.ppermute(ring[-1], 'tensor', [(dev, (dev + 1) % 4) for dev in range(4)])]
    reduce_scatter x1, waiting for transfers between devices: 102 us -> 0.87 us  [body(): lax.psum_scatter(jnp.einsum('jl,rj->lr', in_rows, left, preferred_element...]
    all_gather x1 -> x0, waiting for transfers between devices: 80.4 us -> none  [body(): out_rows = lax.all_gather(basis_out, 'tensor', axis=1, tiled=True)]
    ppermute x0 -> x3, starting transfers between devices: none -> 36.1 us  [body(): lax.ppermute(ring[-1], 'tensor', [(dev, (dev + 1) % 4) for dev in range(4)])]
    reduce_scatter x1, waiting for transfers between devices: 78.3 us -> 93.2 us  [body(): lax.psum_scatter(jnp.einsum('ik,xi->kx', out_rows, right, preferred_eleme...]
    unnamed x15 -> x23, local copies, waits for them, and re-layouts: 5.69 us -> 18.5 us
  transfers between devices with their start and end apart: 8 -> 10, of which waited for: 6 -> 8; matrix products, arithmetic and copies ran while one was open for 4% -> 7% of each run, Pallas kernels for 0% -> 0%
where the time goes in v1:
time: 470 us; the launch traced here: 469 us
  waiting for transfers between devices  311 us (66%)
  blocking collectives  40.5 us (9%)
  starting transfers between devices  37.9 us (8%)
  local copies, waits for them, and re-layouts  33.3 us (7%)
  matrix products  25.7 us (5%)
  between operations  17.3 us (4%)
    ppermute x3, waiting for transfers between devices, body(): lax.ppermute(ring[-1], 'tensor', [(dev, (dev + 1) % 4) for dev in range(4)])  113 us
    reduce_scatter x1, waiting for transfers between devices, body(): lax.psum_scatter(jnp.einsum('ik,xi->kx', out_rows, right, preferred_eleme...  93.2 us
    all_gather x1, waiting for transfers between devices, body(): in_rows = lax.all_gather(basis_in, 'example', axis=1, tiled=True)  60.6 us
    psum x1, blocking collectives, body(): summed = lax.psum(jnp.stack(partial), ('tensor', 'example'))  40.5 us
    ppermute x3, starting transfers between devices, body(): lax.ppermute(ring[-1], 'tensor', [(dev, (dev + 1) % 4) for dev in range(4)])  36.1 us
    all_gather x1, waiting for transfers between devices, body(): acts_rot = lax.all_gather(half_rotated[:, split:], 'example', axis=0)  25.8 us
    unnamed x23, local copies, waits for them, and re-layouts  18.5 us
    all_gather x1, waiting for transfers between devices, body(): grads_rot = lax.all_gather(core[:, query_total * wide:], 'tensor', axis=0)  16.5 us
  transfers between devices with their start and end apart: 10, of which 8 were waited for; matrix products, arithmetic and copies ran while one was open for 7% of the time, Pallas kernels for 0%

profile of v1, /device:TPU:0, one launch (start us, length us, event | category | flops | bytes accessed | tf_op | source)
XLA Modules:
  0.0 469.4 jit_solution(11210910966735715808)
XLA Ops:
  6.5 0.7 all-gather.6.cloned.1.call-update
  7.3 60.6 %all-gather.6.cloned.1.call-done = bf16[1024,4096]{1,0:T(8,128)(2,1)} async-done(((bf16[1024,512]{1,0:T(8,128)(2,1)}), bf16[1024,4096]{1,0:T(8,128)(2,1)}) %all-gather.6.cloned.1.call-update) | async-done | bytes 8388624 | tf_op jit(solution)/shard_map/all_gather | solution.py:42
  67.9 9.8 %fusion = bf16[4096,640]{0,1:T(8,128)(2,1)} fusion(bf16[1024,4096]{1,0:T(8,128)(2,1)} %all-gather.6.cloned.1.call-done, bf16[128,1024]{1,0:T(8,128)(2,1)} %bitcast.47, bf16[512,1024]{1,0:T(8,128)(2,1)} %bitcast.46), kind=kOutput, calls=%fused_computation.2 | convolution fusion | flops 5373952000 | bytes 14942208 | tf_op jit(solution)/shard_map/jl,rj->lr/dot_general | solution.py:54
  77.8 1.1 copy-done.1
  79.0 1.5 collective-permute-start
  80.5 44.6 %collective-permute-done = bf16[512,1024]{1,0:T(8,128)(2,1)S(1)} collective-permute-done((bf16[512,1024]{1,0:T(8,128)(2,1)S(1)}, bf16[512,1024]{1,0:T(8,128)(2,1)S(1)}, u32[]{:S(2)}, u32[]{:S(2)}) %collective-permute-start) | collective-permute-done | bytes 1048608 | tf_op jit(solution)/shard_map/ppermute | solution.py:46
  125.0 17.2 %collective-permute-start.1 = (bf16[512,1024]{1,0:T(8,128)(2,1)S(1)}, bf16[512,1024]{1,0:T(8,128)(2,1)S(1)}, u32[]{:S(2)}, u32[]{:S(2)}) collective-permute-start(bf16[512,1024]{1,0:T(8,128)(2,1)S(1)} %collective-permute-done), channel_id=1, source_target_pairs={{0,8},{8,16},{16,24},{24,0},{1,9},{9,17},{17,25},{25,1},{2,10},{10... | collective-permute-start | bytes 3145736 | tf_op jit(solution)/shard_map/ppermute | solution.py:46
  142.2 48.4 %collective-permute-done.1 = bf16[512,1024]{1,0:T(8,128)(2,1)S(1)} collective-permute-done((bf16[512,1024]{1,0:T(8,128)(2,1)S(1)}, bf16[512,1024]{1,0:T(8,128)(2,1)S(1)}, u32[]{:S(2)}, u32[]{:S(2)}) %collective-permute-start.1) | collective-permute-done | bytes 1048608 | tf_op jit(solution)/shard_map/ppermute | solution.py:46
  190.6 17.4 %collective-permute-start.2 = (bf16[512,1024]{1,0:T(8,128)(2,1)S(1)}, bf16[512,1024]{1,0:T(8,128)(2,1)}, u32[]{:S(2)}, u32[]{:S(2)}) collective-permute-start(bf16[512,1024]{1,0:T(8,128)(2,1)S(1)} %collective-permute-done.1), channel_id=1, source_target_pairs={{0,8},{8,16},{16,24},{24,0},{1,9},{9,17},{17,25},{25,1},{2,10},{10... | collective-permute-start | bytes 3145736 | tf_op jit(solution)/shard_map/ppermute | solution.py:46
  208.0 1.0 constant_dynamic-slice_fusion
  209.0 0.1 copy.26
  209.1 1.3 collective-permute-start.3
  210.5 0.1 copy.27
  210.6 0.1 collective-permute-start.4
  210.7 0.6 fusion.23
  215.3 1.0 fusion.17
  216.4 20.0 %collective-permute-done.2 = bf16[512,1024]{1,0:T(8,128)(2,1)} collective-permute-done((bf16[512,1024]{1,0:T(8,128)(2,1)S(1)}, bf16[512,1024]{1,0:T(8,128)(2,1)}, u32[]{:S(2)}, u32[]{:S(2)}) %collective-permute-start.2) | collective-permute-done | bytes 1048608 | tf_op jit(solution)/shard_map/ppermute | solution.py:46
  236.3 2.3 constant_dynamic-update-slice_fusion.7
  238.7 1.1 constant_dynamic-update-slice_fusion.6
  239.8 1.1 constant_dynamic-update-slice_fusion.5
  240.8 1.1 constant_dynamic-update-slice_fusion.4
  241.9 2.3 constant_dynamic-update-slice_fusion.3
  244.2 1.1 constant_dynamic-update-slice_fusion.2
  245.3 1.1 constant_dynamic-update-slice_fusion.1
  246.4 1.1 constant_dynamic-update-slice_fusion
  247.5 0.9 reduce-scatter.3.cloned.1.call-done
  248.3 1.3 slice.24
  249.6 11.7 %convolution_convert_fusion = bf16[4096,1280]{1,0:T(8,128)(2,1)} fusion(bf16[512,8192]{1,0:T(8,128)(2,1)} %constant_dynamic-update-slice_fusion, s32[]{:T(128)S(6)} %select_n.85, bf16[128,512]{0,1:T(8,128)(2,1)S(1)} %get-tuple-element.8, bf16[128,512]{0,1:T(8,128)(2,1)S(1)} %get-tuple-element.7, bf16[1024,512]{0,1:T(8,128)(2,1)S(1)} %slice.24), kind=kOutput, calls=%fused_computation | convolution fusion | flops 5377884160 | bytes 15990788 | tf_op jit(solution)/shard_map/ik,xi->kx/dot_general | solution.py:64
  261.4 0.0 all-gather.10.cloned.1.call-start
  261.5 1.8 slice.27
  263.3 0.2 all-gather.8.cloned.1.call-start
  263.5 93.2 %reduce-scatter.5.cloned.1.call-done = bf16[512,1280]{1,0:T(8,128)(2,1)} async-done(((bf16[4096,1280]{1,0:T(8,128)(2,1)}), bf16[512,1280]{1,0:T(8,128)(2,1)}) %reduce-scatter.5.cloned.1.call-update) | async-done | bytes 1310736 | tf_op jit(solution)/shard_map/reduce_scatter | solution.py:63
  356.8 1.7 slice.26
  358.5 1.9 copy.21
  360.3 0.2 select_reduce_fusion.2
  360.5 0.1 iota_compare_fusion
  360.6 25.8 %all-gather.10.cloned.1.call-done = bf16[8192,128]{0,1:T(8,128)(2,1)} async-done(((bf16[1024,128]{0,1:T(8,128)(2,1)}), bf16[8192,128]{0,1:T(8,128)(2,1)}) %all-gather.10.cloned.1.call-update) | async-done | bytes 2097168 | tf_op jit(solution)/shard_map/all_gather | solution.py:60
  386.4 2.0 convert_element_type.34
  388.4 5.2 %copy.28 = f32[16,8,8,1024]{3,2,1,0:T(8,128)} copy(f32[16,8,8,1024]{3,1,2,0:T(8,128)S(1)} %bitcast.39) | data formatting | bytes 8388608
  393.7 5.6 %copy.23 = f32[1024,8,128]{2,1,0:T(8,128)} copy(f32[1024,8,128]{0,1,2:T(8,128)} %bitcast.40) | data formatting | bytes 8388608 | tf_op jit(solution)/shard_map/convert_element_type | solution.py:71
  399.3 16.5 %all-gather.8.cloned.1.call-done = bf16[2048,256]{1,0:T(8,128)(2,1)} async-done(((bf16[512,256]{1,0:T(8,128)(2,1)}), bf16[2048,256]{1,0:T(8,128)(2,1)}) %all-gather.8.cloned.1.call-update) | async-done | bytes 1048592 | tf_op jit(solution)/shard_map/all_gather | solution.py:70
  415.8 1.5 copy.22
  417.3 4.2 fusion.1
  421.5 0.1 broadcast_in_dim.58
  421.6 40.5 %psum.7 = f32[128,8]{1,0:T(8,128)S(1)} all-reduce(f32[128,8]{1,0:T(8,128)S(1)} %broadcast_in_dim.58), channel_id=1, replica_groups=mesh['tensor'=4,'example'=8] {'tensor','example'}, use_global_device_ids=true, to_apply=%region_5.6 | all-reduce | flops 1024 | bytes 8192 | tf_op jit(solution)/shard_map/psum | solution.py:78
  462.1 0.1 select_reduce_fusion
  462.2 0.1 copy.25
  462.3 0.6 bitcast_select_fusion
  (23 shorter events, 0.2 us)
Async XLA Ops:
  6.5 353.8 %copy-start = (s32[8,16]{1,0:T(8,128)S(1)}, s32[8,16]{1,0:T(8,128)}, u32[]{:S(2)}) copy-start(s32[8,16]{1,0:T(8,128)} %param.16) | copy-start | bytes 1540
  6.5 61.4 %all-gather.6.cloned.1.call-start = ((), (), s32[]{:S(2)}) async-start(), calls=%async_computation.2 | async-start | bytes 9437184 | tf_op jit(solution)/shard_map/all_gather | solution.py:42
  7.3 241.1 %reduce-scatter.3.cloned.1.call-start = ((), (), s32[]{:S(2)}) async-start(), calls=%async_computation.3 | async-start | bytes 6553600 | tf_op jit(solution)/shard_map/reduce_scatter | solution.py:53
  77.8 1.2 copy-start.1
  77.8 279.0 %reduce-scatter.5.cloned.1.call-start = ((), (), s32[]{:S(2)}) async-start(), calls=%async_computation.4 | async-start | bytes 11796480 | tf_op jit(solution)/shard_map/reduce_scatter | solution.py:63
  79.0 46.0 %collective-permute-start = (bf16[512,1024]{1,0:T(8,128)(2,1)S(1)}, bf16[512,1024]{1,0:T(8,128)(2,1)S(1)}, u32[]{:S(2)}, u32[]{:S(2)}) collective-permute-start(bf16[512,1024]{1,0:T(8,128)(2,1)S(1)} %copy-done.1), channel_id=1, source_target_pairs={{0,8},{8,16},{16,24},{24,0},{1,9},{9,17},{17,25},{25,1},{2,10},{10... | collective-permute-start | bytes 3145736 | tf_op jit(solution)/shard_map/ppermute | solution.py:46
  125.0 65.6 %collective-permute-start.1 = (bf16[512,1024]{1,0:T(8,128)(2,1)S(1)}, bf16[512,1024]{1,0:T(8,128)(2,1)S(1)}, u32[]{:S(2)}, u32[]{:S(2)}) collective-permute-start(bf16[512,1024]{1,0:T(8,128)(2,1)S(1)} %collective-permute-done), channel_id=1, source_target_pairs={{0,8},{8,16},{16,24},{24,0},{1,9},{9,17},{17,25},{25,1},{2,10},{10... | collective-permute-start | bytes 3145736 | tf_op jit(solution)/shard_map/ppermute | solution.py:46
  190.6 45.7 %collective-permute-start.2 = (bf16[512,1024]{1,0:T(8,128)(2,1)S(1)}, bf16[512,1024]{1,0:T(8,128)(2,1)}, u32[]{:S(2)}, u32[]{:S(2)}) collective-permute-start(bf16[512,1024]{1,0:T(8,128)(2,1)S(1)} %collective-permute-done.1), channel_id=1, source_target_pairs={{0,8},{8,16},{16,24},{24,0},{1,9},{9,17},{17,25},{25,1},{2,10},{10... | collective-permute-start | bytes 3145736 | tf_op jit(solution)/shard_map/ppermute | solution.py:46
  209.1 6.2 %collective-permute-start.3 = (bf16[128,512]{0,1:T(8,128)(2,1)S(1)}, bf16[128,512]{0,1:T(8,128)(2,1)}, u32[]{:S(2)}, u32[]{:S(2)}) collective-permute-start(bf16[128,512]{0,1:T(8,128)(2,1)S(1)} %copy.26), channel_id=1, source_target_pairs={{0,0},{1,1},{2,8},{3,9},{4,16},{5,17},{6,24},{7,25},{8,2},{9,3},{1... | collective-permute-start | bytes 393224 | tf_op jit(solution)/shard_map/ppermute | solution.py:22
  210.6 4.7 %collective-permute-start.4 = (bf16[128,512]{0,1:T(8,128)(2,1)S(1)}, bf16[128,512]{0,1:T(8,128)(2,1)S(1)}, u32[]{:S(2)}, u32[]{:S(2)}) collective-permute-start(bf16[128,512]{0,1:T(8,128)(2,1)S(1)} %copy.27), channel_id=1, source_target_pairs={{0,1},{1,0},{2,9},{3,8},{4,17},{5,16},{6,25},{7,24},{8,3},{9,2},{1... | collective-permute-start | bytes 393224 | tf_op jit(solution)/shard_map/ppermute | solution.py:22
  261.4 97.1 %copy-start.2 = (f32[1024,512]{1,0:T(8,128)S(1)}, f32[1024,512]{1,0:T(8,128)}, u32[]{:S(2)}) copy-start(f32[1024,512]{1,0:T(8,128)} %param.12) | copy-start | bytes 6291460
  261.4 98.9 %copy-start.4 = (s32[128]{0:T(128)S(1)}, s32[128]{0:T(128)}, u32[]{:S(2)}) copy-start(s32[128]{0:T(128)} %param.17) | copy-start | bytes 1540
  261.4 98.9 %copy-start.5 = (s32[128]{0:T(128)S(1)}, s32[128]{0:T(128)}, u32[]{:S(2)}) copy-start(s32[128]{0:T(128)} %param.15) | copy-start | bytes 1540
  261.4 125.0 %all-gather.10.cloned.1.call-start = ((), (), s32[]{:S(2)}) async-start(), calls=%async_computation.6 | async-start | bytes 2359296 | tf_op jit(solution)/shard_map/all_gather | solution.py:60
  263.3 152.5 %all-gather.8.cloned.1.call-start = ((), (), s32[]{:S(2)}) async-start(), calls=%async_computation.5 | async-start | bytes 1310720 | tf_op jit(solution)/shard_map/all_gather | solution.py:70
  393.7 23.6 %copy-start.3 = (f32[1024,512]{0,1:T(8,128)S(1)}, f32[1024,512]{0,1:T(8,128)}, u32[]{:S(2)}) copy-start(f32[1024,512]{0,1:T(8,128)} %copy.21) | copy-start | bytes 6291460
Sparse Core Ops, SparseCore 0:
  9.2 58.6 all-gather.5
  77.9 170.3 reduce-scatter.2
  261.5 95.1 reduce-scatter.4
  358.5 27.8 all-gather.9
  387.8 27.9 all-gather.7
